TPU v7x, 256 devices: a whole 4x4x8 slice. The times are simulated.
256 devices in a mesh: gx: 32 (over y, x, core), gz: 8 (over z).
Axes of the slice: x: 4, y: 4, z: 8, core: 2. Of those that a mesh axis runs over, the one named last changes fastest.
Arguments:
- velocity: float32 [64, 3, 128, 64, 256], P(None, None, 'gx', 'gz'), may hold values from -40 to 40
- scaled_modes: float32 [64, 128, 64, 256], P(None, 'gx', 'gz'), may hold values from -70 to 70
Outputs:
- orthonormal: float32 [128, 128, 64, 256], P(None, 'gx', 'gz')
- triangle: float32 [128, 128], replicated
- lower_one: float32 [128, 128], replicated
All inputs are finite; a program needn't handle non-finite values.
Results may differ from a plain program's by a relative error of at most 0.0003.
Values sent between devices are 32-bit elements; how exact they have to be, the bound alone decides.
No kernel may reach another device: no remote copies, remote signals or barrier semaphores. Data moves between devices by JAX's collectives and lax.ppermute only.
A program may use at most 128 MiB of HBM per device.

v0:
```python
import jax
import jax.numpy as jnp
from jax import lax
from jax.sharding import PartitionSpec as P

precise = lax.Precision.HIGHEST


def with_halo(block, sides, width):
    for axis, dim in sides:
        count = lax.axis_size(axis)
        forward = [(i, i + 1) for i in range(count - 1)]
        forward.append((count - 1, 0))
        backward = [(target, source) for source, target in forward]
        low = lax.ppermute(
            lax.slice_in_dim(block, block.shape[dim] - width, None, axis=dim), axis, forward
        )
        high = lax.ppermute(lax.slice_in_dim(block, 0, width, axis=dim), axis, backward)
        block = jnp.concatenate([low, block, high], axis=dim)
    return block


def along_wall(field):
    inner = (field[..., 2:] - field[..., :-2]) * 0.5
    bottom = (-3.0 * field[..., 0:1] + 4.0 * field[..., 1:2] - field[..., 2:3]) * 0.5
    top_side = (3.0 * field[..., -1:] - 4.0 * field[..., -2:-1] + field[..., -3:-2]) * 0.5
    return jnp.concatenate([bottom, inner, top_side], -1)


def product(left, right):
    return lax.dot_general(left, right, (((1,), (1,)), ((), ())), precision=precise)


def shards(velocity, scaled_modes):
    snapshots, _, cells_x, cells_z, cells_y = velocity.shape
    columns_old = scaled_modes.shape[0]
    total_cells = cells_x * lax.axis_size("gx") * cells_z * lax.axis_size("gz") * cells_y
    mode_fields = scaled_modes.reshape(columns_old, -1)
    padded = with_halo(velocity, (("gx", 2), ("gz", 3)), 1)
    grad_x = (padded[:, :, 2:, 1:-1] - padded[:, :, :-2, 1:-1]) * 0.5
    grad_z = (padded[:, :, 1:-1, 2:] - padded[:, :, 1:-1, :-2]) * 0.5
    grad_y = along_wall(velocity)
    diagonal_part = (
        grad_x[:, 0] * grad_x[:, 0] + grad_z[:, 1] * grad_z[:, 1] + grad_y[:, 2] * grad_y[:, 2]
    )
    cross_part = (
        grad_z[:, 0] * grad_x[:, 1] + grad_y[:, 0] * grad_x[:, 2] + grad_y[:, 1] * grad_z[:, 2]
    )
    new_fields = (-0.5 * diagonal_part - cross_part).reshape(snapshots, -1)
    stacked = jnp.concatenate([mode_fields, new_fields], 0)
    gram_sum = lax.psum(product(stacked, stacked), ("gx", "gz"))
    lower_one = jnp.linalg.cholesky(gram_sum / total_cells)
    first_pass = lax.linalg.triangular_solve(lower_one, stacked, left_side=True, lower=True)
    second_sum = lax.psum(product(first_pass, first_pass), ("gx", "gz"))
    lower_two = jnp.linalg.cholesky(second_sum / total_cells)
    basis = lax.linalg.triangular_solve(lower_two, first_pass, left_side=True, lower=True)
    triangle = jnp.dot(lower_two.T, lower_one.T, precision=precise)
    return (basis.reshape(stacked.shape[0], cells_x, cells_z, cells_y), triangle, lower_one)


def solution(mesh):
    in_specs = (P(None, None, "gx", "gz", None), P(None, "gx", "gz", None))
    out_specs = (P(None, "gx", "gz", None), P(), P())
    return jax.shard_map(shards, mesh=mesh, in_specs=in_specs, out_specs=out_specs, check_vma=False)
```

profile of v0, /device:TPU:1, one launch (start us, length us, event | category | flops | bytes accessed | tf_op | source)
XLA Modules:
  0.0 683.3 jit_solution(10335882637036311948)
XLA Ops:
  7.2 0.0 all-reduce.3.cloned.1.call-start
  7.2 6.4 copy.45
  13.7 2.7 copy-done.1
  16.3 2.0 fusion.33
  18.3 2.6 collective-permute-start.1
  20.9 0.6 collective-permute-start
  21.5 7.7 %fusion.32 = (f32[64,3,4,8,1]{4,3,2,1,0:T(8,128)}, f32[64,3,4,8,1]{4,3,2,1,0:T(8,128)}, f32[64,3,4,8,1]{4,3,2,1,0:T(8,128)}, f32[64,3,4,8,1]{4,3,2,1,0:T(8,128)}...) fusion(f32[64,3,4,8,256]{4,3,2,1,0:T(8,128)S(1)} %copy-done), kind=kLoop, calls=%fused_computation.59 | loop fusion | bytes 294912 | tf_op jit(solution)/shard_map/slice | solution.py:25
  29.2 2.7 copy.66
  31.9 2.7 copy.67
  34.6 2.7 copy.68
  37.2 2.7 copy.69
  39.9 2.7 copy.70
  42.6 1.4 copy.71
  44.0 2.3 copy.57
  46.3 2.5 copy.58
  48.8 2.5 copy.72
  51.3 9.2 %fusion = f32[64,3,4,8,254]{4,0,3,2,1:T(8,128)} fusion(f32[64,3,4,8,256]{4,0,3,2,1:T(8,128)} %copy-done.1), kind=kLoop, calls=%fused_computation.1 | loop fusion | flops 3121152 | bytes 18726912 | tf_op jit(solution)/shard_map/mul | solution.py:24
  60.5 7.3 %pad_maximum_fusion.4 = f32[64,3,4,8,256]{4,0,3,2,1:T(8,128)S(1)} fusion(f32[64,3,4,8,1]{4,0,3,2,1:T(8,128)} %copy.58, f32[64,3,4,8,254]{4,0,3,2,1:T(8,128)} %fusion, f32[64,3,4,8,1]{4,0,3,2,1:T(8,128)} %copy.57), kind=kLoop, calls=%fused_computation.10 | loop fusion | flops 3145728 | bytes 12582912 | tf_op jit(solution)/shard_map/concatenate | solution.py:27
  67.8 0.0 collective-permute-done.1
  67.8 1.5 constant_dynamic-update-slice_fusion.2
  69.3 4.1 constant_dynamic-update-slice_fusion.1
  73.4 0.0 collective-permute-done
  73.4 0.0 slice-start.2
  73.4 1.7 constant_dynamic-update-slice_fusion
  75.1 0.0 slice-start.3
  75.1 0.2 fusion.31
  75.3 5.2 collective-permute-start.2
  80.5 1.5 constant_dynamic-update-slice_fusion.4
  82.0 12.6 %fusion.4 = f32[64,3,4,8,256]{4,0,3,2,1:T(8,128)S(1)} fusion(f32[64,3,4,8,256]{4,0,3,2,1:T(8,128)S(1)} %bitcast.38, f32[64,3,1,8,256]{4,0,3,2,1:T(8,128)} %collective-permute-done.1, f32[64,3,1,8,256]{4,0,3,2,1:T(8,128)} %collective-permute-done), kind=kLoop, calls=%fused_computation.8 | loop fusion | flops 6291456 | bytes 15728640 | tf_op jit(solution)/shard_map/mul | solution.py:40
  94.5 7.4 %collective-permute-done.2 = f32[64,3,6,1,256]{4,0,3,2,1:T(8,128)S(1)} collective-permute-done((f32[64,3,6,1,256]{4,0,3,2,1:T(8,128)S(1)}, f32[64,3,6,1,256]{4,0,3,2,1:T(8,128)S(1)}, u32[]{:S(2)}, u32[]{:S(2)}) %collective-permute-start.2) | collective-permute-done | bytes 1179680 | tf_op jit(solution)/shard_map/ppermute | solution.py:18
  102.0 3.1 collective-permute-done.3
  105.1 2.1 fusion.2
  107.2 2.0 fusion.6
  109.3 2.6 copy.59
  111.8 1.7 reshape.49
  113.6 1.5 constant_dynamic-update-slice_fusion.3
  115.0 7.6 %fusion.34 = f32[128,128]{0,1:T(8,128)} fusion(f32[128,8192]{1,0:T(8,128)} %constant_dynamic-update-slice_fusion.3), kind=kOutput, calls=%fused_computation.61 | convolution fusion | flops 1610612736 | bytes 4259840 | tf_op jit(solution)/shard_map/dot_general | solution.py:31
  122.6 0.0 all-reduce.3.cloned.1.call-update
  122.7 0.0 all-reduce.5.cloned.1.call-start
  122.7 243.7 %all-reduce.3.cloned.1.call-done = f32[128,128]{0,1:T(8,128)} async-done(((f32[128,128]{0,1:T(8,128)}), f32[128,128]{0,1:T(8,128)}) %all-reduce.3.cloned.1.call-update) | async-done | bytes 65552 | tf_op jit(solution)/shard_map/psum | solution.py:51
  366.4 0.8 broadcast_multiply_fusion.1
  367.2 0.1 copy.61
  367.3 0.9 fusion.16
  368.2 11.7 %cholesky.44 = f32[128,128]{1,0:T(8,128)S(1)} custom-call(f32[128,128]{1,0:T(8,128)S(1)} %fusion.16), custom_call_target="Cholesky" | custom-call | tf_op jit(solution)/shard_map/jit(cholesky)/cholesky | solution.py:52
  379.9 0.6 compare_reduce_fusion.1
  380.6 0.7 fusion.20
  381.3 0.0 copy-start.5
  381.3 9.8 %custom-call.6 = f32[1,128,128]{1,2,0:T(8,128)S(1)} custom-call(f32[1,128,128]{2,1,0:T(8,128)S(1)} %get-tuple-element.5), custom_call_target="InvertDiagBlocksLowerTriangular" | custom-call | tf_op jit(solution)/shard_map/triangular_solve/custom-call.0 | solution.py:53
  391.1 5.7 fusion.14
  396.7 0.0 copy-start.2
  396.8 2.0 copy-done.2
  398.8 4.0 fusion.35
  402.8 0.0 all-reduce.5.cloned.1.call-update
  402.8 237.9 %all-reduce.5.cloned.1.call-done = f32[128,128]{0,1:T(8,128)} async-done(((f32[128,128]{0,1:T(8,128)}), f32[128,128]{0,1:T(8,128)}) %all-reduce.5.cloned.1.call-update) | async-done | bytes 65552 | tf_op jit(solution)/shard_map/psum | solution.py:54
  640.7 0.8 broadcast_multiply_fusion
  641.6 0.1 copy.63
  641.6 0.9 fusion.13
  642.5 11.7 %cholesky.55 = f32[128,128]{1,0:T(8,128)S(1)} custom-call(f32[128,128]{1,0:T(8,128)S(1)} %fusion.13), custom_call_target="Cholesky" | custom-call | tf_op jit(solution)/shard_map/jit(cholesky)/cholesky | solution.py:55
  654.3 0.7 compare_reduce_fusion
  654.9 0.6 select_bitcast_fusion
  655.6 1.6 fusion.23
  657.1 9.8 %custom-call.7 = f32[1,128,128]{1,2,0:T(8,128)S(1)} custom-call(f32[1,128,128]{2,1,0:T(8,128)S(1)} %select_bitcast_fusion), custom_call_target="InvertDiagBlocksLowerTriangular" | custom-call | tf_op jit(solution)/shard_map/triangular_solve/custom-call.0 | solution.py:56
  667.0 5.7 fusion.11
  672.7 3.3 copy.73
  (21 shorter events, 0.1 us)
Async XLA Ops:
  7.2 359.2 %all-reduce.3.cloned.1.call-start = ((), (), s32[]{:S(2)}) async-start(), calls=%async_computation | async-start | bytes 131072 | tf_op jit(solution)/shard_map/psum | solution.py:51
  13.6 2.7 copy-start.1
  16.3 5.2 copy-start
  18.3 49.5 %collective-permute-start.1 = (f32[64,3,1,8,256]{4,0,3,2,1:T(8,128)}, f32[64,3,1,8,256]{4,0,3,2,1:T(8,128)}, u32[]{:S(2)}, u32[]{:S(2)}) collective-permute-start(f32[64,3,1,8,256]{4,0,3,2,1:T(8,128)} %get-tuple-element.16), channel_id=1, source_target_pairs={{0,8},{8,16},{16,24},{24,32},{32,40},{40,48},{48,56},{56,64},{64,7... | collective-permute-start | bytes 4718600 | tf_op jit(solution)/shard_map/ppermute | solution.py:15
  20.9 52.5 %collective-permute-start = (f32[64,3,1,8,256]{4,0,3,2,1:T(8,128)}, f32[64,3,1,8,256]{4,0,3,2,1:T(8,128)}, u32[]{:S(2)}, u32[]{:S(2)}) collective-permute-start(f32[64,3,1,8,256]{4,0,3,2,1:T(8,128)} %get-tuple-element.15), channel_id=1, source_target_pairs={{8,0},{16,8},{24,16},{32,24},{40,32},{48,40},{56,48},{64,56},{72,6... | collective-permute-start | bytes 4718600 | tf_op jit(solution)/shard_map/ppermute | solution.py:18
  44.0 4.8 copy-start.4
  51.3 18.0 %slice-start = ((s8[6291456]{0:T(1024)(128)(4,1)}), s8[4194304]{0:T(1024)(128)(4,1)S(1)}, s32[]{:S(2)}) async-start(s8[6291456]{0:T(1024)(128)(4,1)} %bitcast.35), calls=%async_computation.2 | async-start | bytes 8388608
  60.5 8.8 %slice-start.1 = ((s8[6291456]{0:T(1024)(128)(4,1)}), s8[2097152]{0:T(1024)(128)(4,1)S(1)}, s32[]{:S(2)}) async-start(s8[6291456]{0:T(1024)(128)(4,1)} %bitcast.35), calls=%async_computation.3 | async-start | bytes 4194304
  73.4 7.1 %copy-start.3 = (f32[8,8,32,256]{3,1,2,0:T(8,128)S(1)}, f32[8,8,32,256]{3,1,2,0:T(8,128)}, u32[]{:S(2)}) copy-start(f32[8,8,32,256]{3,1,2,0:T(8,128)} %copy.72) | copy-start | bytes 6291460
  73.4 8.6 %slice-start.2 = ((s8[6291456]{0:T(1024)(128)(4,1)}), s8[4194304]{0:T(1024)(128)(4,1)S(1)}, s32[]{:S(2)}) async-start(s8[6291456]{0:T(1024)(128)(4,1)} %bitcast.37), calls=%async_computation.4 | async-start | bytes 8388608
  75.1 6.9 %slice-start.3 = ((s8[6291456]{0:T(1024)(128)(4,1)}), s8[2097152]{0:T(1024)(128)(4,1)S(1)}, s32[]{:S(2)}) async-start(s8[6291456]{0:T(1024)(128)(4,1)} %bitcast.37), calls=%async_computation.5 | async-start | bytes 4194304
  75.3 26.6 %collective-permute-start.2 = (f32[64,3,6,1,256]{4,0,3,2,1:T(8,128)S(1)}, f32[64,3,6,1,256]{4,0,3,2,1:T(8,128)S(1)}, u32[]{:S(2)}, u32[]{:S(2)}) collective-permute-start(f32[64,3,6,1,256]{4,0,3,2,1:T(8,128)S(1)} %get-tuple-element.7), channel_id=1, source_target_pairs={{1,0},{2,1},{3,2},{4,3},{5,4},{6,5},{7,6},{0,7},{9,8},{10,9},{11,1... | collective-permute-start | bytes 3538952 | tf_op jit(solution)/shard_map/ppermute | solution.py:18
  80.5 24.6 %collective-permute-start.3 = (f32[64,3,6,1,256]{4,0,3,2,1:T(8,128)S(1)}, f32[64,3,6,1,256]{4,0,3,2,1:T(8,128)S(1)}, u32[]{:S(2)}, u32[]{:S(2)}) collective-permute-start(f32[64,3,6,1,256]{4,0,3,2,1:T(8,128)S(1)} %get-tuple-element.8), channel_id=1, source_target_pairs={{0,1},{1,2},{2,3},{3,4},{4,5},{5,6},{6,7},{7,0},{8,9},{9,10},{10,1... | collective-permute-start | bytes 3538952 | tf_op jit(solution)/shard_map/ppermute | solution.py:15
  122.7 518.0 %all-reduce.5.cloned.1.call-start = ((), (), s32[]{:S(2)}) async-start(), calls=%async_computation.1 | async-start | bytes 131072 | tf_op jit(solution)/shard_map/psum | solution.py:54
  381.3 274.3 %copy-start.5 = (f32[128,128]{1,0:T(8,128)}, f32[128,128]{1,0:T(8,128)S(1)}, u32[]{:S(2)}) copy-start(f32[128,128]{1,0:T(8,128)S(1)} %get-tuple-element.6) | copy-start | bytes 196612
  396.7 2.0 copy-start.2
Sparse Core Ops, SparseCore 0:
  122.8 243.5 all-reduce.2
  402.9 237.7 all-reduce.4
where the time goes:
time: 692 us; the launch traced here: 683 us
  waiting for transfers between devices  492 us (71%)
  other arithmetic  82.3 us (12%)
  local copies, waits for them, and re-layouts  61 us (9%)
  matrix products  24.5 us (4%)
  between operations  14.8 us (2%)
  starting transfers between devices  8.45 us (1%)
    psum x1, waiting for transfers between devices, shards(): gram_sum = lax.psum(product(stacked, stacked), ('gx', 'gz'))  244 us
    psum x1, waiting for transfers between devices, shards(): second_sum = lax.psum(product(first_pass, first_pass), ('gx', 'gz'))  238 us
    unnamed x32, local copies, waits for them, and re-layouts  38.8 us
  transfers between devices with their start and end apart: 6, of which 4 were waited for; matrix products, arithmetic and copies ran while one was open for 10% of the time, Pallas kernels for 0%

commit v1 on v0

--- a/solution.py
+++ b/solution.py
@@ -51,7 +51,7 @@
     gram_sum = lax.psum(product(stacked, stacked), ("gx", "gz"))
     lower_one = jnp.linalg.cholesky(gram_sum / total_cells)
     first_pass = lax.linalg.triangular_solve(lower_one, stacked, left_side=True, lower=True)
-    second_sum = lax.psum(product(first_pass, first_pass), ("gx", "gz"))
+    second_sum = lax.psum(lax.psum(product(first_pass, first_pass), "gx"), "gz")
     lower_two = jnp.linalg.cholesky(second_sum / total_cells)
     basis = lax.linalg.triangular_solve(lower_two, first_pass, left_side=True, lower=True)
     triangle = jnp.dot(lower_two.T, lower_one.T, precision=precise)

time: 692 us -> 629 us (0.909)
  the two profiles are of different devices: /device:TPU:1 before, /device:TPU:2 now
where the time goes in v1:
time: 629 us; the launch traced here: 621 us
  waiting for transfers between devices  440 us (70%)
  other arithmetic  72.6 us (12%)
  local copies, waits for them, and re-layouts  61.1 us (10%)
  matrix products  24.1 us (4%)
  between operations  14.2 us (2%)
  starting transfers between devices  8.38 us (1%)
    psum x1, waiting for transfers between devices, shards(): gram_sum = lax.psum(product(stacked, stacked), ('gx', 'gz'))  238 us
    psum x2, waiting for transfers between devices, shards(): second_sum = lax.psum(lax.psum(product(first_pass, first_pass), 'gx'), 'gz')  178 us
    unnamed x32, local copies, waits for them, and re-layouts  38.9 us
    ppermute x2, waiting for transfers between devices, with_halo(): lax.ppermute(lax.slice_in_dim(block, 0, width, axis=dim), axis, backward)  20.9 us
  transfers between devices with their start and end apart: 7, of which 5 were waited for; matrix products, arithmetic and copies ran while one was open for 9% of the time, Pallas kernels for 0%

profile of v1, /device:TPU:2, one launch (start us, length us, event | category | flops | bytes accessed | tf_op | source)
XLA Modules:
  0.0 620.6 jit_solution(11998191761671767725)
XLA Ops:
  7.2 0.0 all-reduce.4.cloned.1.call-start
  7.2 6.4 %copy.45 = f32[64,3,4,8,256]{4,0,3,2,1:T(8,128)S(1)} copy(f32[64,3,4,8,256]{4,3,2,1,0:T(8,128)} %param.5) | data formatting | bytes 12582912 | tf_op args[0]
  13.7 2.7 copy-done.1
  16.3 2.0 fusion.33
  18.3 1.7 collective-permute-start
  20.1 0.2 copy-done
  20.2 7.7 %fusion.32 = (f32[64,3,4,8,1]{4,3,2,1,0:T(8,128)}, f32[64,3,4,8,1]{4,3,2,1,0:T(8,128)}, f32[64,3,4,8,1]{4,3,2,1,0:T(8,128)}, f32[64,3,4,8,1]{4,3,2,1,0:T(8,128)}...) fusion(f32[64,3,4,8,256]{4,3,2,1,0:T(8,128)S(1)} %copy-done), kind=kLoop, calls=%fused_computation.59 | loop fusion | bytes 294912 | tf_op jit(solution)/shard_map/slice | solution.py:25
  27.9 2.7 copy.66
  30.6 2.7 copy.67
  33.2 2.7 copy.68
  35.9 2.7 copy.69
  38.6 2.7 copy.70
  41.2 1.4 copy.71
  42.7 2.3 copy.57
  45.0 2.4 copy.58
  47.4 2.5 copy.72
  49.9 9.2 %fusion = f32[64,3,4,8,254]{4,0,3,2,1:T(8,128)} fusion(f32[64,3,4,8,256]{4,0,3,2,1:T(8,128)} %copy-done.1), kind=kLoop, calls=%fused_computation.1 | loop fusion | flops 3121152 | bytes 18726912 | tf_op jit(solution)/shard_map/mul | solution.py:24
  59.1 7.3 %pad_maximum_fusion.4 = f32[64,3,4,8,256]{4,0,3,2,1:T(8,128)S(1)} fusion(f32[64,3,4,8,1]{4,0,3,2,1:T(8,128)} %copy.58, f32[64,3,4,8,254]{4,0,3,2,1:T(8,128)} %fusion, f32[64,3,4,8,1]{4,0,3,2,1:T(8,128)} %copy.57), kind=kLoop, calls=%fused_computation.10 | loop fusion | flops 3145728 | bytes 12582912 | tf_op jit(solution)/shard_map/concatenate | solution.py:27
  66.4 0.0 collective-permute-done.1
  66.4 1.5 constant_dynamic-update-slice_fusion.2
  67.9 4.1 constant_dynamic-update-slice_fusion.1
  72.0 1.7 constant_dynamic-update-slice_fusion
  73.7 0.2 fusion.31
  73.9 5.9 collective-permute-start.2
  79.9 1.5 constant_dynamic-update-slice_fusion.4
  81.4 2.8 fusion.4
  84.2 20.9 %collective-permute-done.2 = f32[64,3,6,1,256]{4,0,3,2,1:T(8,128)S(1)} collective-permute-done((f32[64,3,6,1,256]{4,0,3,2,1:T(8,128)S(1)}, f32[64,3,6,1,256]{4,0,3,2,1:T(8,128)S(1)}, u32[]{:S(2)}, u32[]{:S(2)}) %collective-permute-start.2) | collective-permute-done | bytes 1179680 | tf_op jit(solution)/shard_map/ppermute | solution.py:18
  105.1 3.4 collective-permute-done.3
  108.5 2.1 fusion.2
  110.6 2.0 fusion.6
  112.7 2.6 copy.59
  115.2 1.7 reshape.49
  117.0 1.5 constant_dynamic-update-slice_fusion.3
  118.4 7.6 %fusion.34 = f32[128,128]{0,1:T(8,128)} fusion(f32[128,8192]{1,0:T(8,128)} %constant_dynamic-update-slice_fusion.3), kind=kOutput, calls=%fused_computation.61 | convolution fusion | flops 1610612736 | bytes 4259840 | tf_op jit(solution)/shard_map/dot_general | solution.py:31
  126.0 0.0 all-reduce.4.cloned.1.call-update
  126.1 0.4 all-reduce.6.cloned.1.call-start
  126.5 237.7 %all-reduce.4.cloned.1.call-done = f32[128,128]{0,1:T(8,128)} async-done(((f32[128,128]{0,1:T(8,128)}), f32[128,128]{0,1:T(8,128)}) %all-reduce.4.cloned.1.call-update) | async-done | bytes 65552 | tf_op jit(solution)/shard_map/psum | solution.py:51
  364.3 0.8 broadcast_multiply_fusion.1
  365.1 0.1 copy.61
  365.2 0.9 fusion.16
  366.1 11.7 %cholesky.44 = f32[128,128]{1,0:T(8,128)S(1)} custom-call(f32[128,128]{1,0:T(8,128)S(1)} %fusion.16), custom_call_target="Cholesky" | custom-call | tf_op jit(solution)/shard_map/jit(cholesky)/cholesky | solution.py:52
  377.8 0.6 compare_reduce_fusion.1
  378.5 0.7 fusion.20
  379.1 0.0 copy-start.5
  379.1 9.8 %custom-call.6 = f32[1,128,128]{1,2,0:T(8,128)S(1)} custom-call(f32[1,128,128]{2,1,0:T(8,128)S(1)} %get-tuple-element.5), custom_call_target="InvertDiagBlocksLowerTriangular" | custom-call | tf_op jit(solution)/shard_map/triangular_solve/custom-call.0 | solution.py:53
  388.9 5.4 fusion.14
  394.4 0.0 copy-start.2
  394.4 2.0 copy-done.2
  396.4 4.0 fusion.35
  400.5 0.0 all-reduce.6.cloned.1.call-update
  400.5 0.2 all-reduce.8.cloned.1.call-start
  400.7 103.7 %all-reduce.6.cloned.1.call-done = f32[128,128]{0,1:T(8,128)} async-done(((f32[128,128]{0,1:T(8,128)}), f32[128,128]{0,1:T(8,128)}) %all-reduce.6.cloned.1.call-update) | async-done | bytes 65552 | tf_op jit(solution)/shard_map/psum | solution.py:54
  504.4 0.0 all-reduce.8.cloned.1.call-update
  504.5 74.4 %all-reduce.8.cloned.1.call-done = f32[128,128]{0,1:T(8,128)} async-done(((f32[128,128]{0,1:T(8,128)}), f32[128,128]{0,1:T(8,128)}) %all-reduce.8.cloned.1.call-update) | async-done | bytes 65552 | tf_op jit(solution)/shard_map/psum | solution.py:54
  578.9 0.8 broadcast_multiply_fusion
  579.7 0.1 copy.63
  579.8 0.9 fusion.13
  580.7 11.7 %cholesky.55 = f32[128,128]{1,0:T(8,128)S(1)} custom-call(f32[128,128]{1,0:T(8,128)S(1)} %fusion.13), custom_call_target="Cholesky" | custom-call | tf_op jit(solution)/shard_map/jit(cholesky)/cholesky | solution.py:55
  592.4 0.7 compare_reduce_fusion
  593.1 0.6 select_bitcast_fusion
  593.8 1.6 fusion.23
  595.3 9.8 %custom-call.7 = f32[1,128,128]{1,2,0:T(8,128)S(1)} custom-call(f32[1,128,128]{2,1,0:T(8,128)S(1)} %select_bitcast_fusion), custom_call_target="InvertDiagBlocksLowerTriangular" | custom-call | tf_op jit(solution)/shard_map/triangular_solve/custom-call.0 | solution.py:56
  605.1 5.4 fusion.11
  610.6 3.3 copy.73
  (24 shorter events, 0.1 us)
Async XLA Ops:
  7.2 357.1 %all-reduce.4.cloned.1.call-start = ((), (), s32[]{:S(2)}) async-start(), calls=%async_computation | async-start | bytes 131072 | tf_op jit(solution)/shard_map/psum | solution.py:51
  13.6 2.7 copy-start.1
  16.3 3.9 copy-start
  18.3 48.1 %collective-permute-start.1 = (f32[64,3,1,8,256]{4,0,3,2,1:T(8,128)}, f32[64,3,1,8,256]{4,0,3,2,1:T(8,128)}, u32[]{:S(2)}, u32[]{:S(2)}) collective-permute-start(f32[64,3,1,8,256]{4,0,3,2,1:T(8,128)} %get-tuple-element.16), channel_id=1, source_target_pairs={{0,8},{8,16},{16,24},{24,32},{32,40},{40,48},{48,56},{56,64},{64,7... | collective-permute-start | bytes 4718600 | tf_op jit(solution)/shard_map/ppermute | solution.py:15
  18.3 53.7 %collective-permute-start = (f32[64,3,1,8,256]{4,0,3,2,1:T(8,128)}, f32[64,3,1,8,256]{4,0,3,2,1:T(8,128)}, u32[]{:S(2)}, u32[]{:S(2)}) collective-permute-start(f32[64,3,1,8,256]{4,0,3,2,1:T(8,128)} %get-tuple-element.15), channel_id=1, source_target_pairs={{8,0},{16,8},{24,16},{32,24},{40,32},{48,40},{56,48},{64,56},{72,6... | collective-permute-start | bytes 4718600 | tf_op jit(solution)/shard_map/ppermute | solution.py:18
  42.7 4.7 copy-start.4
  49.9 18.0 %slice-start = ((s8[6291456]{0:T(1024)(128)(4,1)}), s8[4194304]{0:T(1024)(128)(4,1)S(1)}, s32[]{:S(2)}) async-start(s8[6291456]{0:T(1024)(128)(4,1)} %bitcast.35), calls=%async_computation.3 | async-start | bytes 8388608
  59.1 8.8 %slice-start.1 = ((s8[6291456]{0:T(1024)(128)(4,1)}), s8[2097152]{0:T(1024)(128)(4,1)S(1)}, s32[]{:S(2)}) async-start(s8[6291456]{0:T(1024)(128)(4,1)} %bitcast.35), calls=%async_computation.4 | async-start | bytes 4194304
  72.0 7.9 %copy-start.3 = (f32[8,8,32,256]{3,1,2,0:T(8,128)S(1)}, f32[8,8,32,256]{3,1,2,0:T(8,128)}, u32[]{:S(2)}) copy-start(f32[8,8,32,256]{3,1,2,0:T(8,128)} %copy.72) | copy-start | bytes 6291460
  72.0 9.3 %slice-start.2 = ((s8[6291456]{0:T(1024)(128)(4,1)}), s8[4194304]{0:T(1024)(128)(4,1)S(1)}, s32[]{:S(2)}) async-start(s8[6291456]{0:T(1024)(128)(4,1)} %bitcast.37), calls=%async_computation.5 | async-start | bytes 8388608
  73.7 7.6 %slice-start.3 = ((s8[6291456]{0:T(1024)(128)(4,1)}), s8[2097152]{0:T(1024)(128)(4,1)S(1)}, s32[]{:S(2)}) async-start(s8[6291456]{0:T(1024)(128)(4,1)} %bitcast.37), calls=%async_computation.6 | async-start | bytes 4194304
  73.9 31.2 %collective-permute-start.2 = (f32[64,3,6,1,256]{4,0,3,2,1:T(8,128)S(1)}, f32[64,3,6,1,256]{4,0,3,2,1:T(8,128)S(1)}, u32[]{:S(2)}, u32[]{:S(2)}) collective-permute-start(f32[64,3,6,1,256]{4,0,3,2,1:T(8,128)S(1)} %get-tuple-element.7), channel_id=1, source_target_pairs={{1,0},{2,1},{3,2},{4,3},{5,4},{6,5},{7,6},{0,7},{9,8},{10,9},{11,1... | collective-permute-start | bytes 3538952 | tf_op jit(solution)/shard_map/ppermute | solution.py:18
  79.9 28.6 %collective-permute-start.3 = (f32[64,3,6,1,256]{4,0,3,2,1:T(8,128)S(1)}, f32[64,3,6,1,256]{4,0,3,2,1:T(8,128)S(1)}, u32[]{:S(2)}, u32[]{:S(2)}) collective-permute-start(f32[64,3,6,1,256]{4,0,3,2,1:T(8,128)S(1)} %get-tuple-element.8), channel_id=1, source_target_pairs={{0,1},{1,2},{2,3},{3,4},{4,5},{5,6},{6,7},{7,0},{8,9},{9,10},{10,1... | collective-permute-start | bytes 3538952 | tf_op jit(solution)/shard_map/ppermute | solution.py:15
  126.1 378.4 %all-reduce.6.cloned.1.call-start = ((), (), s32[]{:S(2)}) async-start(), calls=%async_computation.1 | async-start | bytes 131072 | tf_op jit(solution)/shard_map/psum | solution.py:54
  379.1 214.7 %copy-start.5 = (f32[128,128]{1,0:T(8,128)}, f32[128,128]{1,0:T(8,128)S(1)}, u32[]{:S(2)}) copy-start(f32[128,128]{1,0:T(8,128)S(1)} %get-tuple-element.6) | copy-start | bytes 196612
  394.4 2.0 copy-start.2
  400.5 178.4 %all-reduce.8.cloned.1.call-start = ((), (), s32[]{:S(2)}) async-start(), calls=%async_computation.2 | async-start | bytes 131072 | tf_op jit(solution)/shard_map/psum | solution.py:54
Sparse Core Ops, SparseCore 0:
  126.2 238.0 all-reduce.3
  400.6 103.7 all-reduce.5
  506.7 72.1 all-reduce.7
